TPU v7x, 256 devices: a whole 4x4x8 slice. The times are simulated.
256 devices in a mesh: dp: 8 (over y, x_lo), tensor: 32 (over x_hi, z, core).
Axes of the slice: x: 4 (x_hi: 2, x_lo: 2; x = x_hi * 2 + x_lo), y: 4, z: 8, core: 2. Of those that a mesh axis runs over, the one named last changes fastest.
Arguments:
- hidden: bfloat16 [6144, 20480], P('dp', 'tensor'), may hold values from -6 to 6
- out_grad: bfloat16 [6144, 8192], P('dp', 'tensor'), may hold values from -6 to 6
- w_down: bfloat16 [20480, 8192], P('tensor'), may hold values from -0.0625 to 0.0625
- proj_in: bfloat16 [64, 20480], P(None, 'tensor'), may hold values from -0.0390625 to 0.0390625
- proj_out: bfloat16 [64, 8192], P(None, 'tensor'), may hold values from -0.0625 to 0.0625
- queries: bfloat16 [1024, 4096], P('tensor'), may hold values from -0.005859375 to 0.005859375
- assignment: int32 [24], replicated, may hold values from 0 to 15
Outputs:
- input_grad: bfloat16 [6144, 20480], P('dp', 'tensor')
- scores: float32 [16, 1024], P('dp', 'tensor')
All inputs are finite; a program needn't handle non-finite values.
Results may differ from a plain program's by a relative error of at most 0.001.
Values may be sent and summed in bfloat16 or wider, within the bound.
No kernel may reach another device: no remote copies, remote signals or barrier semaphores. Data moves between devices by JAX's collectives and lax.ppermute only.
A program may use at most 128 MiB of HBM per device.

v0:
```python
import jax
import jax.numpy as jnp
from jax import lax
from jax.sharding import PartitionSpec as P

LEN = 256
EX_DEV = 2


def on_device(hidden, out_grad, w_down, proj_in, proj_out, queries, assignment):
    tok_rows = hidden.shape[0]
    seq_count = tok_rows // LEN
    act_part = jnp.einsum("tf,kf->tk", hidden, proj_in, preferred_element_type=jnp.float32)
    grad_piece = lax.all_gather(out_grad, "tensor", axis=1, tiled=True)
    proj_piece = lax.all_gather(proj_out, "tensor", axis=1, tiled=True)
    first = jnp.einsum("td,fd->tf", grad_piece, w_down, preferred_element_type=jnp.float32)
    second = jnp.einsum("td,kd->tk", grad_piece, proj_piece, preferred_element_type=jnp.float32)
    act_low = lax.psum(act_part, "tensor")
    input_grad = first.astype(jnp.bfloat16)
    width = act_low.shape[1]
    act_seq = act_low.reshape(seq_count, LEN, width)
    grad_seq = second.reshape(seq_count, LEN, width)
    proj_grads = jnp.einsum(
        "slk,slm->skm", act_seq, grad_seq, precision=lax.Precision.HIGHEST
    ).reshape(seq_count, width * width)
    query_wide = queries.astype(jnp.float32)
    all_grads = lax.all_gather(proj_grads, "dp", axis=0, tiled=True)
    first_example = lax.axis_index("dp") * EX_DEV
    example_ids = first_example + jnp.arange(EX_DEV, dtype=jnp.int32)
    one_hot = (example_ids[:, None] == assignment[None, :]).astype(jnp.float32)
    example_grads = jnp.dot(one_hot, all_grads, precision=lax.Precision.HIGHEST)
    scores = jnp.dot(example_grads, query_wide.T, precision=lax.Precision.HIGHEST)
    return (input_grad, scores)


def solution(mesh):
    placed = (
        P("dp", "tensor"),
        P("dp", "tensor"),
        P("tensor", None),
        P(None, "tensor"),
        P(None, "tensor"),
        P("tensor", None),
        P(),
    )
    return jax.shard_map(
        on_device,
        mesh=mesh,
        in_specs=placed,
        out_specs=(P("dp", "tensor"), P("dp", "tensor")),
        check_vma=False,
    )
```

profile of v0, /device:TPU:4, one launch (start us, length us, event | category | flops | bytes accessed | tf_op | source)
XLA Modules:
  0.0 524.6 jit_solution(11781420502975008039)
XLA Ops:
  7.2 0.0 copy-start
  7.2 0.0 copy-start.1
  7.2 0.0 copy-start.2
  7.2 0.0 all-gather.6.cloned.1.call-start
  7.2 0.7 all-gather.6.cloned.1.call-update
  7.9 0.0 all-gather.4.cloned.1.call-start
  8.0 0.7 all-gather.4.cloned.1.call-update
  8.7 0.0 all-reduce.2.cloned.1.call-start
  8.7 0.0 copy-done
  8.7 1.3 fusion.7
  10.0 0.7 copy.22
  10.7 0.0 all-reduce.2.cloned.1.call-update
  10.8 73.6 %all-gather.6.cloned.1.call-done = bf16[64,8192]{1,0:T(8,128)(2,1)} async-done(((bf16[64,256]{1,0:T(8,128)(2,1)}), bf16[64,8192]{1,0:T(8,128)(2,1)}) %all-gather.6.cloned.1.call-update) | async-done | bytes 1048592 | tf_op jit(solution)/shard_map/all_gather | solution.py:15
  84.3 129.2 %all-gather.4.cloned.1.call-done = bf16[768,8192]{1,0:T(8,128)(2,1)} async-done(((bf16[768,256]{1,0:T(8,128)(2,1)}), bf16[768,8192]{1,0:T(8,128)(2,1)}) %all-gather.4.cloned.1.call-update) | async-done | bytes 12582928 | tf_op jit(solution)/shard_map/all_gather | solution.py:14
  213.5 8.7 %fusion.8 = f32[768,64]{0,1:T(8,128)S(1)} fusion(bf16[768,8192]{1,0:T(8,128)(2,1)} %all-gather.4.cloned.1.call-done, bf16[64,8192]{1,0:T(8,128)(2,1)} %all-gather.6.cloned.1.call-done), kind=kOutput, calls=%fused_computation.11 | convolution fusion | flops 805306368 | bytes 13828096 | tf_op jit(solution)/shard_map/td,kd->tk/dot_general | solution.py:17
  222.3 247.4 %all-reduce.2.cloned.1.call-done = f32[3,256,64]{1,2,0:T(8,128)} async-done(((f32[3,256,64]{1,2,0:T(8,128)}), f32[3,256,64]{1,2,0:T(8,128)}) %all-reduce.2.cloned.1.call-update) | async-done | bytes 196624 | tf_op jit(solution)/shard_map/psum | solution.py:18
  469.7 1.2 fusion
  470.9 0.1 reshape.21
  471.0 30.2 %all-gather = f32[8,3,4096]{2,1,0:T(4,128)S(1)} all-gather(f32[1,3,4096]{2,1,0:T(4,128)S(1)} %reshape.21), channel_id=1, replica_groups=mesh['dp'=8,'tensor'=32] {'dp'}, dimensions={0}, use_global_device_ids=true | all-gather | bytes 442368 | tf_op jit(solution)/shard_map/all_gather | solution.py:27
  501.2 0.2 reshape.22
  501.4 0.0 copy-done.1
  501.4 0.3 fusion.3
  501.7 0.0 copy-done.2
  501.7 0.9 fusion.9
  502.6 15.5 %convolution_convert_fusion = bf16[768,640]{1,0:T(8,128)(2,1)} fusion(bf16[768,8192]{1,0:T(8,128)(2,1)} %all-gather.4.cloned.1.call-done, bf16[640,8192]{1,0:T(8,128)(2,1)} %param.9), kind=kOutput, calls=%fused_computation | convolution fusion | flops 8053555200 | bytes 24051712 | tf_op jit(solution)/shard_map/td,fd->tf/dot_general | solution.py:16
  (1 shorter events, 0.0 us)
Async XLA Ops:
  7.2 1.6 copy-start
  7.2 494.2 %copy-start.1 = (s32[24]{0:T(128)S(1)}, s32[24]{0:T(128)}, u32[]{:S(2)}) copy-start(s32[24]{0:T(128)} %param.13) | copy-start | bytes 292
  7.2 494.5 %copy-start.2 = (bf16[32,4096]{1,0:T(8,128)(2,1)S(1)}, bf16[32,4096]{1,0:T(8,128)(2,1)}, u32[]{:S(2)}) copy-start(bf16[32,4096]{1,0:T(8,128)(2,1)} %param.12) | copy-start | bytes 786436
  7.2 77.1 %all-gather.6.cloned.1.call-start = ((), (), s32[]{:S(2)}) async-start(), calls=%async_computation.2 | async-start | bytes 1081344 | tf_op jit(solution)/shard_map/all_gather | solution.py:15
  7.9 205.6 %all-gather.4.cloned.1.call-start = ((), (), s32[]{:S(2)}) async-start(), calls=%async_computation | async-start | bytes 12976128 | tf_op jit(solution)/shard_map/all_gather | solution.py:14
  8.7 461.0 %all-reduce.2.cloned.1.call-start = ((), (), s32[]{:S(2)}) async-start(), calls=%async_computation.1 | async-start | bytes 393216 | tf_op jit(solution)/shard_map/psum | solution.py:18
Sparse Core Ops, SparseCore 0:
  10.6 73.7 all-gather.5
  86.9 126.5 all-gather.3
  216.7 252.9 all-reduce.1
where the time goes:
time: 525 us
  waiting for transfers between devices  452 us (86%)
  blocking collectives  30.2 us (6%)
  matrix products  27.9 us (5%)
  between operations  13.8 us (3%)
    psum x1, waiting for transfers between devices, on_device(): act_low = lax.psum(act_part, 'tensor')  247 us
    all_gather x1, waiting for transfers between devices, on_device(): grad_piece = lax.all_gather(out_grad, 'tensor', axis=1, tiled=True)  129 us
    all_gather x1, waiting for transfers between devices, on_device(): proj_piece = lax.all_gather(proj_out, 'tensor', axis=1, tiled=True)  73.6 us
    all_gather x1, blocking collectives, on_device(): all_grads = lax.all_gather(proj_grads, 'dp', axis=0, tiled=True)  30.2 us
    dot_general x1, matrix products, on_device(): jnp.einsum('td,fd->tf', grad_piece, w_down, preferred_element_type=jnp.fl...  15.5 us
  transfers between devices with their start and end apart: 3, of which 3 were waited for; matrix products, arithmetic and copies ran while one was open for 2% of the time, Pallas kernels for 0%

commit v1 on v0

--- a/solution.py
+++ b/solution.py
@@ -15,7 +15,7 @@
     proj_piece = lax.all_gather(proj_out, "tensor", axis=1, tiled=True)
     first = jnp.einsum("td,fd->tf", grad_piece, w_down, preferred_element_type=jnp.float32)
     second = jnp.einsum("td,kd->tk", grad_piece, proj_piece, preferred_element_type=jnp.float32)
-    act_low = lax.psum(act_part, "tensor")
+    act_low = lax.all_gather(act_part, axis_name="tensor").sum(axis=0)
     input_grad = first.astype(jnp.bfloat16)
     width = act_low.shape[1]
     act_seq = act_low.reshape(seq_count, LEN, width)

time: 525 us -> 373 us (0.71)
  waiting for transfers between devices: 452 us -> 292 us
    psum x1 -> x0, waiting for transfers between devices: 247 us -> none  [on_device(): act_low = lax.psum(act_part, 'tensor')]
    all_gather x0 -> x1, waiting for transfers between devices: none -> 94.5 us  [on_device(): act_low = lax.all_gather(act_part, axis_name='tensor').sum(axis=0)]
    all_gather x1, waiting for transfers between devices: 73.6 us -> 66.9 us  [on_device(): proj_piece = lax.all_gather(proj_out, 'tensor', axis=1, tiled=True)]
    unnamed x8 -> x9, local copies, waits for them, and re-layouts: 0.32 us -> 6.12 us
  transfers between devices with their start and end apart: 3 -> 3, of which waited for: 3 -> 3; matrix products, arithmetic and copies ran while one was open for 2% -> 1% of each run, Pallas kernels for 0% -> 0%
where the time goes in v1:
time: 373 us; the launch traced here: 371 us
  waiting for transfers between devices  292 us (78%)
  blocking collectives  30.2 us (8%)
  matrix products  27.7 us (7%)
  between operations  13.8 us (4%)
  local copies, waits for them, and re-layouts  6.12 us (2%)
    all_gather x1, waiting for transfers between devices, on_device(): grad_piece = lax.all_gather(out_grad, 'tensor', axis=1, tiled=True)  129 us
    all_gather x1, waiting for transfers between devices, on_device(): act_low = lax.all_gather(act_part, axis_name='tensor').sum(axis=0)  94.5 us
    all_gather x1, waiting for transfers between devices, on_device(): proj_piece = lax.all_gather(proj_out, 'tensor', axis=1, tiled=True)  66.9 us
    all_gather x1, blocking collectives, on_device(): all_grads = lax.all_gather(proj_grads, 'dp', axis=0, tiled=True)  30.2 us
    dot_general x1, matrix products, on_device(): jnp.einsum('td,fd->tf', grad_piece, w_down, preferred_element_type=jnp.fl...  15.5 us
    dot_general x1, matrix products, on_device(): jnp.einsum('td,kd->tk', grad_piece, proj_piece, preferred_element_type=jn...  8.72 us
  transfers between devices with their start and end apart: 3, of which 3 were waited for; matrix products, arithmetic and copies ran while one was open for 1% of the time, Pallas kernels for 0%

profile of v1, /device:TPU:4, one launch (start us, length us, event | category | flops | bytes accessed | tf_op | source)
XLA Modules:
  0.0 370.7 jit_solution(8555874523316764895)
XLA Ops:
  7.2 0.0 copy-start
  7.2 0.0 all-gather.10.cloned.1.call-start
  7.2 1.1 copy-done
  8.4 2.0 fusion.9
  10.4 0.0 all-gather.10.cloned.1.call-update
  10.4 0.0 all-gather.8.cloned.1.call-start
  10.4 0.7 all-gather.8.cloned.1.call-update
  11.1 0.0 all-gather.6.cloned.1.call-start
  11.2 0.7 all-gather.6.cloned.1.call-update
  11.9 94.5 %all-gather.10.cloned.1.call-done = f32[24576,64]{0,1:T(8,128)} async-done(((f32[768,64]{0,1:T(8,128)}), f32[24576,64]{0,1:T(8,128)}) %all-gather.10.cloned.1.call-update) | async-done | bytes 6291472 | tf_op jit(solution)/shard_map/all_gather | solution.py:18
  106.3 4.7 %copy.16 = f32[8,8,32,768]{3,2,1,0:T(8,128)S(1)} copy(f32[8,8,32,768]{3,1,2,0:T(8,128)} %bitcast.22) | data formatting | bytes 12582912
  111.0 0.0 copy-start.1
  111.0 0.0 copy-start.2
  111.0 0.9 bitcast_reduce_fusion
  111.9 66.9 %all-gather.8.cloned.1.call-done = bf16[64,8192]{1,0:T(8,128)(2,1)} async-done(((bf16[64,256]{1,0:T(8,128)(2,1)}), bf16[64,8192]{1,0:T(8,128)(2,1)}) %all-gather.8.cloned.1.call-update) | async-done | bytes 1048592 | tf_op jit(solution)/shard_map/all_gather | solution.py:15
  178.8 129.2 %all-gather.6.cloned.1.call-done = bf16[768,8192]{1,0:T(8,128)(2,1)} async-done(((bf16[768,256]{1,0:T(8,128)(2,1)}), bf16[768,8192]{1,0:T(8,128)(2,1)}) %all-gather.6.cloned.1.call-update) | async-done | bytes 12582928 | tf_op jit(solution)/shard_map/all_gather | solution.py:14
  308.0 8.7 %fusion.10 = f32[768,64]{0,1:T(8,128)S(1)} fusion(bf16[768,8192]{1,0:T(8,128)(2,1)} %all-gather.6.cloned.1.call-done, bf16[64,8192]{1,0:T(8,128)(2,1)} %all-gather.8.cloned.1.call-done), kind=kOutput, calls=%fused_computation.13 | convolution fusion | flops 805306368 | bytes 13828096 | tf_op jit(solution)/shard_map/td,kd->tk/dot_general | solution.py:17
  316.7 0.3 fusion
  317.1 0.1 reshape.22
  317.2 30.2 %all-gather.1 = f32[8,3,4096]{2,1,0:T(4,128)S(1)} all-gather(f32[1,3,4096]{2,1,0:T(4,128)S(1)} %reshape.22), channel_id=1, replica_groups=mesh['dp'=8,'tensor'=32] {'dp'}, dimensions={0}, use_global_device_ids=true | all-gather | bytes 442368 | tf_op jit(solution)/shard_map/all_gather | solution.py:27
  347.3 0.2 reshape.23
  347.5 0.0 copy-done.1
  347.6 0.3 fusion.5
  347.8 0.0 copy-done.2
  347.8 0.9 fusion.11
  348.7 15.5 %convolution_convert_fusion = bf16[768,640]{1,0:T(8,128)(2,1)} fusion(bf16[768,8192]{1,0:T(8,128)(2,1)} %all-gather.6.cloned.1.call-done, bf16[640,8192]{1,0:T(8,128)(2,1)} %param.9), kind=kOutput, calls=%fused_computation.1 | convolution fusion | flops 8053555200 | bytes 24051712 | tf_op jit(solution)/shard_map/td,fd->tf/dot_general | solution.py:16
  (1 shorter events, 0.0 us)
Async XLA Ops:
  7.2 1.2 copy-start
  7.2 99.2 %all-gather.10.cloned.1.call-start = ((), (), s32[]{:S(2)}) async-start(), calls=%async_computation.2 | async-start | bytes 6488064 | tf_op jit(solution)/shard_map/all_gather | solution.py:18
  10.4 168.4 %all-gather.8.cloned.1.call-start = ((), (), s32[]{:S(2)}) async-start(), calls=%async_computation.1 | async-start | bytes 1081344 | tf_op jit(solution)/shard_map/all_gather | solution.py:15
  11.1 296.9 %all-gather.6.cloned.1.call-start = ((), (), s32[]{:S(2)}) async-start(), calls=%async_computation | async-start | bytes 12976128 | tf_op jit(solution)/shard_map/all_gather | solution.py:14
  111.0 236.5 %copy-start.1 = (s32[24]{0:T(128)S(1)}, s32[24]{0:T(128)}, u32[]{:S(2)}) copy-start(s32[24]{0:T(128)} %param.13) | copy-start | bytes 292
  111.0 236.8 %copy-start.2 = (bf16[32,4096]{1,0:T(8,128)(2,1)S(1)}, bf16[32,4096]{1,0:T(8,128)(2,1)}, u32[]{:S(2)}) copy-start(bf16[32,4096]{1,0:T(8,128)(2,1)} %param.12) | copy-start | bytes 786436
Sparse Core Ops, SparseCore 0:
  11.3 95.0 all-gather.9
  108.9 69.8 all-gather.7
  181.4 126.5 all-gather.5

commit v2 on v0

--- a/solution.py
+++ b/solution.py
@@ -7,11 +7,18 @@
 EX_DEV = 2
 
 
+def bind_the_node(mine, ax_name):
+    met_up = jnp.concatenate(
+        lax.all_to_all(jnp.stack(lax.psum(1, ax_name) * [mine]), ax_name, 0, 0), axis=1
+    )
+    return met_up
+
+
 def on_device(hidden, out_grad, w_down, proj_in, proj_out, queries, assignment):
     tok_rows = hidden.shape[0]
     seq_count = tok_rows // LEN
     act_part = jnp.einsum("tf,kf->tk", hidden, proj_in, preferred_element_type=jnp.float32)
-    grad_piece = lax.all_gather(out_grad, "tensor", axis=1, tiled=True)
+    grad_piece = bind_the_node(out_grad, "tensor")
     proj_piece = lax.all_gather(proj_out, "tensor", axis=1, tiled=True)
     first = jnp.einsum("td,fd->tf", grad_piece, w_down, preferred_element_type=jnp.float32)
     second = jnp.einsum("td,kd->tk", grad_piece, proj_piece, preferred_element_type=jnp.float32)

time: 525 us -> 487 us (0.928)
  waiting for transfers between devices: 452 us -> 358 us
  local copies, waits for them, and re-layouts: 1.02 us -> 44.7 us
  starting transfers between devices: 0.11 us -> 11.9 us
    all_to_all x0 -> x1, waiting for transfers between devices: none -> 279 us  [bind_the_node(): lax.all_to_all(jnp.stack(lax.psum(1, ax_name) * [mine]), ax_name, 0, 0)]
    psum x1, waiting for transfers between devices: 247 us -> 78 us  [on_device(): act_low = lax.psum(act_part, 'tensor')]
    all_gather x1 -> x0, waiting for transfers between devices: 129 us -> none  [on_device(): grad_piece = lax.all_gather(out_grad, 'tensor', axis=1, tiled=True)]
    all_gather x1, waiting for transfers between devices: 73.6 us -> 0.01 us  [on_device(): proj_piece = lax.all_gather(proj_out, 'tensor', axis=1, tiled=True)]
    dot_general x0 -> x1, local copies, waits for them, and re-layouts: none -> 19.6 us  [on_device(): jnp.einsum('td,kd->tk', grad_piece, proj_piece, preferred_element_type=jn...]
    reshape x0 -> x1, local copies, waits for them, and re-layouts: none -> 17 us  [bind_the_node(): jnp.concatenate(lax.all_to_all(jnp.stack(lax.psum(1, ax_name) * [mine]),...]
    all_to_all x0 -> x1, starting transfers between devices: none -> 11.8 us  [bind_the_node(): lax.all_to_all(jnp.stack(lax.psum(1, ax_name) * [mine]), ax_name, 0, 0)]
    another operation x0 -> x1, local copies, waits for them, and re-layouts: none -> 5.9 us  [bind_the_node(): jnp.stack(lax.psum(1, ax_name) * [mine])]
  transfers between devices with their start and end apart: 3 -> 3, of which waited for: 3 -> 2; matrix products, arithmetic and copies ran while one was open for 2% -> 10% of each run, Pallas kernels for 0% -> 0%
where the time goes in v2:
time: 487 us; the launch traced here: 486 us
  waiting for transfers between devices  358 us (74%)
  local copies, waits for them, and re-layouts  44.7 us (9%)
  blocking collectives  30.2 us (6%)
  matrix products  27.1 us (6%)
  between operations  14.1 us (3%)
  starting transfers between devices  11.9 us (2%)
    all_to_all x1, waiting for transfers between devices, bind_the_node(): lax.all_to_all(jnp.stack(lax.psum(1, ax_name) * [mine]), ax_name, 0, 0)  279 us
    psum x1, waiting for transfers between devices, on_device(): act_low = lax.psum(act_part, 'tensor')  78 us
    all_gather x1, blocking collectives, on_device(): all_grads = lax.all_gather(proj_grads, 'dp', axis=0, tiled=True)  30.2 us
    dot_general x1, local copies, waits for them, and re-layouts, on_device(): jnp.einsum('td,kd->tk', grad_piece, proj_piece, preferred_element_type=jn...  19.6 us
    reshape x1, local copies, waits for them, and re-layouts, bind_the_node(): jnp.concatenate(lax.all_to_all(jnp.stack(lax.psum(1, ax_name) * [mine]),...  17 us
    dot_general x1, matrix products, on_device(): jnp.einsum('td,fd->tf', grad_piece, w_down, preferred_element_type=jnp.fl...  15.5 us
    all_to_all x1, starting transfers between devices, bind_the_node(): lax.all_to_all(jnp.stack(lax.psum(1, ax_name) * [mine]), ax_name, 0, 0)  11.8 us
  transfers between devices with their start and end apart: 3, of which 2 were waited for; matrix products, arithmetic and copies ran while one was open for 10% of the time, Pallas kernels for 0%

profile of v2, /device:TPU:4, one launch (start us, length us, event | category | flops | bytes accessed | tf_op | source)
XLA Modules:
  0.0 486.0 jit_solution(8541443015016455069)
XLA Ops:
  7.2 0.0 copy-start
  7.2 1.2 copy.13
  8.4 5.9 %stack.2 = bf16[32,768,256]{1,2,0:T(8,128)(2,1)} broadcast(bf16[768,256]{0,1:T(8,128)(2,1)S(1)} %copy.13), dimensions={1,2} | broadcast | bytes 12976128 | tf_op jit(solution)/shard_map/stack | solution.py:12
  14.3 0.0 copy-start.1
  14.3 11.8 %all-to-all-start = ((bf16[32,768,256]{1,2,0:T(8,128)(2,1)}), bf16[32,768,256]{1,2,0:T(8,128)(2,1)}, u32[]{:S(2)}, u32[]{:S(2)}) async-start(bf16[32,768,256]{1,2,0:T(8,128)(2,1)} %stack.2), calls=%async_computation | async-start | bytes 25165824 | tf_op jit(solution)/shard_map/all_to_all | solution.py:12
  26.1 0.0 all-gather.3.cloned.1.call-start
  26.2 0.7 all-gather.3.cloned.1.call-update
  26.9 0.0 all-reduce.2.cloned.1.call-start
  26.9 0.0 copy-done
  26.9 0.0 copy-done.1
  26.9 0.4 fusion.6
  27.3 0.7 copy.18
  28.0 0.0 all-reduce.2.cloned.1.call-update
  28.1 279.3 %all-to-all-done = bf16[32,768,256]{1,2,0:T(8,128)(2,1)} async-done(((bf16[32,768,256]{1,2,0:T(8,128)(2,1)}), bf16[32,768,256]{1,2,0:T(8,128)(2,1)}, u32[]{:S(2)}, u32[]{:S(2)}) %all-to-all-start) | async-done | bytes 12582944 | tf_op jit(solution)/shard_map/all_to_all | solution.py:12
  307.4 17.0 %copy.15 = bf16[768,32,256]{2,1,0:T(8,128)(2,1)} copy(bf16[768,32,256]{0,2,1:T(8,128)(2,1)} %bitcast) | data formatting | bytes 25165824 | tf_op jit(solution)/shard_map/reshape | solution.py:11
  324.4 19.6 %dot_general.22 = bf16[3,256,8192]{2,1,0:T(8,128)(2,1)} reshape(bf16[768,32,256]{2,1,0:T(8,128)(2,1)} %copy.15) | data formatting | bytes 25165824 | tf_op jit(solution)/shard_map/td,kd->tk/dot_general | solution.py:24
  343.9 0.0 all-gather.3.cloned.1.call-done
  343.9 8.7 %fusion = f32[3,256,64]{1,2,0:T(8,128)S(1)} fusion(bf16[3,256,8192]{2,1,0:T(8,128)(2,1)} %dot_general.22, bf16[64,8192]{1,0:T(8,128)(2,1)} %all-gather.3.cloned.1.call-done), kind=kOutput, calls=%fused_computation.1 | convolution fusion | flops 805306368 | bytes 13828096 | tf_op jit(solution)/shard_map/td,kd->tk/dot_general | solution.py:24
  352.7 78.0 %all-reduce.2.cloned.1.call-done = f32[3,256,64]{1,2,0:T(8,128)} async-done(((f32[3,256,64]{1,2,0:T(8,128)}), f32[3,256,64]{1,2,0:T(8,128)}) %all-reduce.2.cloned.1.call-update) | async-done | bytes 196624 | tf_op jit(solution)/shard_map/psum | solution.py:25
  430.7 1.2 fusion.7
  431.9 0.1 reshape.30
  432.0 30.2 %all-gather = f32[8,3,4096]{2,1,0:T(4,128)S(1)} all-gather(f32[1,3,4096]{2,1,0:T(4,128)S(1)} %reshape.30), channel_id=1, replica_groups=mesh['dp'=8,'tensor'=32] {'dp'}, dimensions={0}, use_global_device_ids=true | all-gather | bytes 442368 | tf_op jit(solution)/shard_map/all_gather | solution.py:34
  462.2 0.2 reshape.31
  462.4 0.0 copy-start.2
  462.4 0.0 copy-start.3
  462.4 15.5 %convolution_convert_fusion = bf16[768,640]{1,0:T(8,128)(2,1)} fusion(bf16[768,8192]{0,1:T(8,128)(2,1)} %bitcast.1, bf16[640,8192]{1,0:T(8,128)(2,1)} %param.9), kind=kOutput, calls=%fused_computation | convolution fusion | flops 8053555200 | bytes 24051712 | tf_op jit(solution)/shard_map/td,fd->tf/dot_general | solution.py:23
  478.0 0.0 copy-done.2
  478.0 0.3 fusion.2
  478.3 0.0 copy-done.3
  478.3 0.9 fusion.8
  (1 shorter events, 0.0 us)
Async XLA Ops:
  7.2 19.7 %copy-start = (bf16[768,640]{1,0:T(8,128)(2,1)S(1)}, bf16[768,640]{1,0:T(8,128)(2,1)}, u32[]{:S(2)}) copy-start(bf16[768,640]{1,0:T(8,128)(2,1)} %param.7) | copy-start | bytes 2949124
  14.3 12.6 %copy-start.1 = (bf16[64,640]{1,0:T(8,128)(2,1)S(1)}, bf16[64,640]{1,0:T(8,128)(2,1)}, u32[]{:S(2)}) copy-start(bf16[64,640]{1,0:T(8,128)(2,1)} %param.10) | copy-start | bytes 245764
  14.3 293.0 %all-to-all-start = ((bf16[32,768,256]{1,2,0:T(8,128)(2,1)}), bf16[32,768,256]{1,2,0:T(8,128)(2,1)}, u32[]{:S(2)}, u32[]{:S(2)}) async-start(bf16[32,768,256]{1,2,0:T(8,128)(2,1)} %stack.2), calls=%async_computation | async-start | bytes 25165824 | tf_op jit(solution)/shard_map/all_to_all | solution.py:12
  26.1 317.8 %all-gather.3.cloned.1.call-start = ((), (), s32[]{:S(2)}) async-start(), calls=%async_computation.2 | async-start | bytes 1081344 | tf_op jit(solution)/shard_map/all_gather | solution.py:22
  26.9 403.8 %all-reduce.2.cloned.1.call-start = ((), (), s32[]{:S(2)}) async-start(), calls=%async_computation.1 | async-start | bytes 393216 | tf_op jit(solution)/shard_map/psum | solution.py:25
  462.4 15.6 %copy-start.2 = (s32[24]{0:T(128)S(1)}, s32[24]{0:T(128)}, u32[]{:S(2)}) copy-start(s32[24]{0:T(128)} %param.13) | copy-start | bytes 292
  462.4 15.8 %copy-start.3 = (bf16[32,4096]{1,0:T(8,128)(2,1)S(1)}, bf16[32,4096]{1,0:T(8,128)(2,1)}, u32[]{:S(2)}) copy-start(bf16[32,4096]{1,0:T(8,128)(2,1)} %param.12) | copy-start | bytes 786436
Sparse Core Ops, SparseCore 0:
  29.5 112.8 all-gather.2
  145.6 285.0 all-reduce.1
